TPU v7x, 256 devices: a whole 4x4x8 slice. The times are simulated.
256 devices in a mesh: seq: 64 (over x, z_lo, y, core), tensor: 4 (over z_hi).
Axes of the slice: x: 4, y: 4, z: 8 (z_hi: 4, z_lo: 2; z = z_hi * 2 + z_lo), core: 2. Of those that a mesh axis runs over, the one named last changes fastest.
Arguments:
- q_tok: bfloat16 [32768, 1536], P('seq', 'tensor'), may hold values from -24 to 24
- k_tok: bfloat16 [32768, 1536], P('seq', 'tensor'), may hold values from -6 to 6
- v_tok: bfloat16 [32768, 1536], P('seq', 'tensor'), may hold values from -16 to 16
- ref_hidden: bfloat16 [2048, 3072], P('seq', 'tensor'), may hold values from -16 to 16
- ref_wk: bfloat16 [3072, 1536], P('tensor'), may hold values from -0.109375 to 0.109375
- ref_wv: bfloat16 [3072, 1536], P('tensor'), may hold values from -0.109375 to 0.109375
- key_gain: float32 [128], replicated, may hold values from 1 to 2
Outputs:
- attended: bfloat16 [32768, 1536], P('seq', 'tensor')
All inputs are finite; a program needn't handle non-finite values.
Results may differ from a plain program's by a relative error of at most 0.022.
Values may be sent and summed in bfloat16 or wider, within the bound.
No kernel may reach another device: no remote copies, remote signals or barrier semaphores. Data moves between devices by JAX's collectives and lax.ppermute only.
A program may use at most 128 MiB of HBM per device.

v0:
```python
import jax
import jax.numpy as jnp
from jax import lax
from jax.sharding import PartitionSpec as P

HD = 128
VIEW_LEN = 4096
EPSILON = 1e-06


def from_partner(block, axis, apart):
    count = lax.axis_size(axis)
    route = []
    for low in range(count):
        high = low | 1 << apart
        if high != low and high < count:
            route += [(low, high), (high, low)]
    return lax.ppermute(block, axis, route)


def attend(carried, queries, key_rows, values):
    running_max, running_sum, weighted = carried
    head_count = queries.shape[1] // HD
    factor = HD ** (-0.5)
    new_maxes, new_sums, new_weighted = ([], [], [])
    for head_index in range(head_count):
        col_start = head_index * HD
        col_stop = col_start + HD
        scores = (
            jnp.einsum(
                "qd,kd->qk",
                queries[:, col_start:col_stop],
                key_rows[:, col_start:col_stop],
                preferred_element_type=jnp.float32,
            )
            * factor
        )
        raised = jnp.maximum(running_max[head_index], jnp.max(scores, axis=1))
        rescale = jnp.exp(running_max[head_index] - raised)
        weights = jnp.exp(scores - raised[:, None])
        new_sums.append(running_sum[head_index] * rescale + jnp.sum(weights, axis=1))
        product = jnp.dot(
            weights.astype(jnp.bfloat16),
            values[:, col_start:col_stop],
            preferred_element_type=jnp.float32,
        )
        new_weighted.append(weighted[:, col_start:col_stop] * rescale[:, None] + product)
        new_maxes.append(raised)
    return (jnp.stack(new_maxes), jnp.stack(new_sums), jnp.concatenate(new_weighted, axis=1))


def reference_pair(ref_hidden, ref_wk, ref_wv, key_gain):
    k_partial = jnp.dot(ref_hidden, ref_wk, preferred_element_type=jnp.float32)
    v_partial = jnp.dot(ref_hidden, ref_wv, preferred_element_type=jnp.float32)
    row_count = ref_hidden.shape[0]
    groups = lax.axis_size("tensor")
    group_width = k_partial.shape[1] // groups
    stacked = jnp.stack(
        (
            k_partial.reshape(row_count, groups, group_width),
            v_partial.reshape(row_count, groups, group_width),
        ),
        axis=2,
    ).reshape(row_count, 2 * groups * group_width)
    summed = lax.psum_scatter(
        stacked.astype(jnp.bfloat16), "tensor", scatter_dimension=1, tiled=True
    ).astype(jnp.float32)
    raw_keys = summed[:, :group_width].reshape(row_count, group_width // HD, HD)
    normed = (
        raw_keys
        * lax.rsqrt(jnp.mean(raw_keys * raw_keys, axis=2, keepdims=True) + EPSILON)
        * key_gain
    )
    return (
        normed.reshape(row_count, group_width).astype(jnp.bfloat16),
        summed[:, group_width:].astype(jnp.bfloat16),
    )


def per_device(q_tok, k_tok, v_tok, ref_hidden, ref_wk, ref_wv, key_gain):
    ref_keys, ref_vals = reference_pair(ref_hidden, ref_wk, ref_wv, key_gain)
    query_rows = q_tok.shape[0]
    heads_here = q_tok.shape[1] // HD
    group_size = VIEW_LEN // query_rows
    view_bits = group_size.bit_length() - 1
    initial = (
        jnp.full((heads_here, query_rows), -jnp.inf, jnp.float32),
        jnp.zeros((heads_here, query_rows), jnp.float32),
        jnp.zeros(q_tok.shape, jnp.float32),
    )
    view_keys, view_vals = (k_tok, v_tok)
    for bit_index in range(view_bits):
        other_keys, other_vals = from_partner((view_keys, view_vals), "seq", bit_index)
        view_keys = jnp.concatenate((view_keys, other_keys), axis=0)
        view_vals = jnp.concatenate((view_vals, other_vals), axis=0)
    carried = attend(initial, q_tok, view_keys, view_vals)
    carried = attend(
        carried,
        q_tok,
        lax.all_gather(ref_keys, "seq", axis=0, tiled=True),
        lax.all_gather(ref_vals, "seq", axis=0, tiled=True),
    )
    running_max, running_sum, weighted = carried
    spread = jnp.repeat(running_sum.T, HD, axis=1)
    return (weighted / spread).astype(jnp.bfloat16)


def solution(mesh):
    placed = (
        P("seq", "tensor"),
        P("seq", "tensor"),
        P("seq", "tensor"),
        P("seq", "tensor"),
        P("tensor", None),
        P("tensor", None),
        P(),
    )
    return jax.shard_map(
        per_device, mesh=mesh, in_specs=placed, out_specs=P("seq", "tensor"), check_vma=False
    )
```

profile of v0, /device:TPU:1, one launch (start us, length us, event | category | flops | bytes accessed | tf_op | source)
XLA Modules:
  0.0 341.4 jit_solution(11778259846070906958)
XLA Ops:
  6.6 1.6 copy-done
  8.2 1.3 convolution_convert_fusion.1
  9.6 2.2 convolution_convert_fusion
  13.2 27.0 %reduce-scatter.2.cloned.1.call-done = bf16[32,768]{1,0:T(8,128)(2,1)} async-done(((bf16[32,3072]{1,0:T(8,128)(2,1)}), bf16[32,768]{1,0:T(8,128)(2,1)}) %reduce-scatter.2.cloned.1.call-update) | async-done | bytes 49168 | tf_op jit(solution)/shard_map/reduce_scatter | solution.py:65
  41.3 1.4 fusion.83
  42.7 3.0 collective-permute-start
  45.7 1.3 collective-permute-done
  47.1 1.3 collective-permute-start.1
  49.1 16.9 %collective-permute-done.1 = bf16[1024,384]{1,0:T(8,128)(2,1)S(1)} collective-permute-done((bf16[1024,384]{1,0:T(8,128)(2,1)S(1)}, bf16[1024,384]{1,0:T(8,128)(2,1)S(1)}, u32[]{:S(2)}, u32[]{:S(2)}) %collective-permute-start.1) | collective-permute-done | bytes 786464 | tf_op jit(solution)/shard_map/ppermute | solution.py:18
  66.0 1.3 pad_maximum_fusion
  67.3 3.8 %collective-permute-start.2 = (bf16[2048,384]{1,0:T(8,128)(2,1)}, bf16[2048,384]{1,0:T(8,128)(2,1)}, u32[]{:S(2)}, u32[]{:S(2)}) collective-permute-start(bf16[2048,384]{1,0:T(8,128)(2,1)} %pad_maximum_fusion), channel_id=1, source_target_pairs={{0,16},{16,0},{4,20},{20,4},{8,24},{24,8},{12,28},{28,12},{32,48},... | collective-permute-start | bytes 4718600 | tf_op jit(solution)/shard_map/ppermute | solution.py:18
  71.1 1.0 pad_maximum_fusion.3
  76.2 45.3 %collective-permute-done.4 = bf16[1024,384]{1,0:T(8,128)(2,1)S(1)} collective-permute-done((bf16[1024,384]{1,0:T(8,128)(2,1)}, bf16[1024,384]{1,0:T(8,128)(2,1)S(1)}, u32[]{:S(2)}, u32[]{:S(2)}) %collective-permute-start.4) | collective-permute-done | bytes 786464 | tf_op jit(solution)/shard_map/ppermute | solution.py:18
  121.7 3.4 collective-permute-start.5
  125.1 1.0 constant_dynamic-update-slice_fusion.1
  127.0 2.7 constant_dynamic-update-slice_fusion
  129.7 2.6 multiply_reduce_fusion
  132.4 1.3 multiply_reduce_fusion.1
  133.7 1.3 multiply_reduce_fusion.2
  135.6 1.5 fusion.4
  137.1 1.1 copy-done.3
  138.2 1.5 fusion.2
  139.6 18.5 %collective-permute-done.5 = bf16[2048,384]{1,0:T(8,128)(2,1)S(1)} collective-permute-done((bf16[2048,384]{1,0:T(8,128)(2,1)S(1)}, bf16[2048,384]{1,0:T(8,128)(2,1)S(1)}, u32[]{:S(2)}, u32[]{:S(2)}) %collective-permute-start.5) | collective-permute-done | bytes 1572896 | tf_op jit(solution)/shard_map/ppermute | solution.py:18
  158.4 1.6 copy-done.17
  160.0 1.4 fusion
  161.5 50.6 %all-gather.3.cloned.1.call-done = bf16[2048,384]{1,0:T(8,128)(2,1)} async-done(((bf16[32,384]{1,0:T(8,128)(2,1)}), bf16[2048,384]{1,0:T(8,128)(2,1)}) %all-gather.3.cloned.1.call-update) | async-done | bytes 1572880 | tf_op jit(solution)/shard_map/all_gather | solution.py:100
  212.1 1.9 multiply_reduce_fusion.3
  219.2 98.7 %all-gather.5.cloned.1.call-done = bf16[2048,384]{1,0:T(8,128)(2,1)} async-done(((bf16[32,384]{1,0:T(8,128)(2,1)}), bf16[2048,384]{1,0:T(8,128)(2,1)}) %all-gather.5.cloned.1.call-update) | async-done | bytes 1572880 | tf_op jit(solution)/shard_map/all_gather | solution.py:101
  318.0 3.3 fusion.18
  321.3 5.3 %fusion.54 = f32[512,128]{0,1:T(8,128)S(1)} fusion(f32[512,128]{0,1:T(8,128)S(1)} %fusion.18, f32[4096,512]{1,0:T(8,128)} %copy-done.4, f32[512]{0:T(512)S(1)} %get-tuple-element.14, bf16[4096,384]{1,0:T(8,128)(2,1)} %copy-done.17, f32[512]{0:T(512)S(1)} %get-tuple-element.9, f32[512]{0:T(512)S(1)} %get-tuple-element.13), kind=kOutput, calls=%fused_computation.48 | convolution fusion | flops 543358976 | bytes 9967616 | tf_op jit(solution)/shard_map/dot_general | solution.py:42
  328.5 1.6 fusion.45
  332.2 1.6 fusion.36
  (93 shorter events, 19.8 us)
Async XLA Ops:
  6.5 6.6 %copy-start.19 = (f32[128]{0:T(128)S(1)}, f32[128]{0:T(128)}, u32[]{:S(2)}) copy-start(f32[128]{0:T(128)} %param.13) | copy-start | bytes 1540
  6.5 36.2 %copy-start.11 = (bf16[512,384]{1,0:T(8,128)(2,1)S(1)}, bf16[512,384]{1,0:T(8,128)(2,1)}, u32[]{:S(2)}) copy-start(bf16[512,384]{1,0:T(8,128)(2,1)} %param.8) | copy-start | bytes 1179652
  6.5 41.9 %copy-start.12 = (bf16[512,384]{1,0:T(8,128)(2,1)S(1)}, bf16[512,384]{1,0:T(8,128)(2,1)}, u32[]{:S(2)}) copy-start(bf16[512,384]{1,0:T(8,128)(2,1)} %param.9) | copy-start | bytes 1179652
  6.5 33.7 %reduce-scatter.2.cloned.1.call-start = ((), (), s32[]{:S(2)}) async-start(), calls=%async_computation.1 | async-start | bytes 245760 | tf_op jit(solution)/shard_map/reduce_scatter | solution.py:65
  13.1 199.0 %all-gather.3.cloned.1.call-start = ((), (), s32[]{:S(2)}) async-start(), calls=%async_computation.2 | async-start | bytes 1597440 | tf_op jit(solution)/shard_map/all_gather | solution.py:100
  40.2 33.8 %copy-start.15 = (bf16[32,768]{1,0:T(8,128)(2,1)S(1)}, bf16[32,768]{1,0:T(8,128)(2,1)}, u32[]{:S(2)}) copy-start(bf16[32,768]{1,0:T(8,128)(2,1)} %reduce-scatter.2.cloned.1.call-done) | copy-start | bytes 147460
  42.7 275.3 %all-gather.5.cloned.1.call-start = ((), (), s32[]{:S(2)}) async-start(), calls=%async_computation.3 | async-start | bytes 1597440 | tf_op jit(solution)/shard_map/all_gather | solution.py:101
  42.7 4.3 %collective-permute-start = (bf16[512,384]{1,0:T(8,128)(2,1)S(1)}, bf16[512,384]{1,0:T(8,128)(2,1)S(1)}, u32[]{:S(2)}, u32[]{:S(2)}) collective-permute-start(bf16[512,384]{1,0:T(8,128)(2,1)S(1)} %copy-done.11), channel_id=1, source_target_pairs={{0,4},{4,0},{8,12},{12,8},{16,20},{20,16},{24,28},{28,24},{32,36},... | collective-permute-start | bytes 1179656 | tf_op jit(solution)/shard_map/ppermute | solution.py:18
  47.1 18.8 %collective-permute-start.1 = (bf16[1024,384]{1,0:T(8,128)(2,1)S(1)}, bf16[1024,384]{1,0:T(8,128)(2,1)S(1)}, u32[]{:S(2)}, u32[]{:S(2)}) collective-permute-start(bf16[1024,384]{1,0:T(8,128)(2,1)S(1)} %pad_maximum_fusion.2), channel_id=1, source_target_pairs={{0,8},{8,0},{4,12},{12,4},{16,24},{24,16},{20,28},{28,20},{32,40},... | collective-permute-start | bytes 2359304 | tf_op jit(solution)/shard_map/ppermute | solution.py:18
  48.4 22.6 %collective-permute-start.3 = (bf16[512,384]{1,0:T(8,128)(2,1)S(1)}, bf16[512,384]{1,0:T(8,128)(2,1)S(1)}, u32[]{:S(2)}, u32[]{:S(2)}) collective-permute-start(bf16[512,384]{1,0:T(8,128)(2,1)S(1)} %copy-done.12), channel_id=1, source_target_pairs={{0,4},{4,0},{8,12},{12,8},{16,20},{20,16},{24,28},{28,24},{32,36},... | collective-permute-start | bytes 1179656 | tf_op jit(solution)/shard_map/ppermute | solution.py:18
  67.3 59.7 %collective-permute-start.2 = (bf16[2048,384]{1,0:T(8,128)(2,1)}, bf16[2048,384]{1,0:T(8,128)(2,1)}, u32[]{:S(2)}, u32[]{:S(2)}) collective-permute-start(bf16[2048,384]{1,0:T(8,128)(2,1)} %pad_maximum_fusion), channel_id=1, source_target_pairs={{0,16},{16,0},{4,20},{20,4},{8,24},{24,8},{12,28},{28,12},{32,48},... | collective-permute-start | bytes 4718600 | tf_op jit(solution)/shard_map/ppermute | solution.py:18
  72.1 49.4 %collective-permute-start.4 = (bf16[1024,384]{1,0:T(8,128)(2,1)}, bf16[1024,384]{1,0:T(8,128)(2,1)S(1)}, u32[]{:S(2)}, u32[]{:S(2)}) collective-permute-start(bf16[1024,384]{1,0:T(8,128)(2,1)} %pad_maximum_fusion.3), channel_id=1, source_target_pairs={{0,8},{8,0},{4,12},{12,4},{16,24},{24,16},{20,28},{28,20},{32,40},... | collective-permute-start | bytes 2359304 | tf_op jit(solution)/shard_map/ppermute | solution.py:18
  76.2 53.5 %copy-start.13 = (bf16[512,384]{1,0:T(8,128)(2,1)S(1)}, bf16[512,384]{1,0:T(8,128)(2,1)}, u32[]{:S(2)}) copy-start(bf16[512,384]{1,0:T(8,128)(2,1)} %param.7) | copy-start | bytes 1179652
  121.7 36.4 %collective-permute-start.5 = (bf16[2048,384]{1,0:T(8,128)(2,1)S(1)}, bf16[2048,384]{1,0:T(8,128)(2,1)S(1)}, u32[]{:S(2)}, u32[]{:S(2)}) collective-permute-start(bf16[2048,384]{1,0:T(8,128)(2,1)S(1)} %pad_maximum_fusion.1), channel_id=1, source_target_pairs={{0,16},{16,0},{4,20},{20,4},{8,24},{24,8},{12,28},{28,12},{32,48},... | collective-permute-start | bytes 4718600 | tf_op jit(solution)/shard_map/ppermute | solution.py:18
  129.7 2.6 copy-start.10
  132.4 3.2 copy-start.4
  133.7 4.5 %copy-start.3 = (f32[4096,512]{1,0:T(8,128)}, f32[4096,512]{1,0:T(8,128)S(1)}, u32[]{:S(2)}) copy-start(f32[4096,512]{1,0:T(8,128)S(1)} %get-tuple-element.19) | copy-start | bytes 25165828
  134.9 25.1 %copy-start.2 = (f32[4096,512]{1,0:T(8,128)}, f32[4096,512]{1,0:T(8,128)S(1)}, u32[]{:S(2)}) copy-start(f32[4096,512]{1,0:T(8,128)S(1)} %get-tuple-element.23) | copy-start | bytes 25165828
  138.2 19.9 %copy-start.16 = (bf16[4096,384]{1,0:T(8,128)(2,1)S(1)}, bf16[4096,384]{1,0:T(8,128)(2,1)}, u32[]{:S(2)}) copy-start(bf16[4096,384]{1,0:T(8,128)(2,1)} %constant_dynamic-update-slice_fusion.5) | copy-start | bytes 9437188
  212.1 1.9 copy-start.14
  214.0 2.1 copy-start.9
  214.7 2.4 copy-start.7
  215.5 3.0 copy-start.5
  317.9 8.7 %copy-start.20 = (bf16[2048,384]{1,0:T(8,128)(2,1)S(1)}, bf16[2048,384]{1,0:T(8,128)(2,1)}, u32[]{:S(2)}) copy-start(bf16[2048,384]{1,0:T(8,128)(2,1)} %all-gather.5.cloned.1.call-done) | copy-start | bytes 4718596
  318.0 9.6 %slice-start.2 = ((s8[8388608]{0:T(1024)(128)(4,1)}), s8[4194304]{0:T(1024)(128)(4,1)S(1)}, s32[]{:S(2)}) async-start(s8[8388608]{0:T(1024)(128)(4,1)} %bitcast.27), calls=%async_computation.6 | async-start | bytes 8388608
  321.3 5.4 %copy-start.8 = (f32[2048,512]{1,0:T(8,128)S(1)}, f32[2048,512]{1,0:T(8,128)}, u32[]{:S(2)}) copy-start(f32[2048,512]{1,0:T(8,128)} %copy-done.7) | copy-start | bytes 12582916
  321.3 6.3 %slice-start.3 = ((s8[8388608]{0:T(1024)(128)(4,1)}), s8[4194304]{0:T(1024)(128)(4,1)S(1)}, s32[]{:S(2)}) async-start(s8[8388608]{0:T(1024)(128)(4,1)} %bitcast.27), calls=%async_computation.7 | async-start | bytes 8388608
  321.3 7.2 %copy-start.18 = (bf16[4096,384]{1,0:T(8,128)(2,1)S(1)}, bf16[4096,384]{1,0:T(8,128)(2,1)}, u32[]{:S(2)}) copy-start(bf16[4096,384]{1,0:T(8,128)(2,1)} %copy-done.17) | copy-start | bytes 9437188
  326.7 5.0 %slice-start = ((s8[8388608]{0:T(1024)(128)(4,1)}), s8[4194304]{0:T(1024)(128)(4,1)S(1)}, s32[]{:S(2)}) async-start(s8[8388608]{0:T(1024)(128)(4,1)} %bitcast.25), calls=%async_computation.4 | async-start | bytes 8388608
  328.5 2.2 copy-start.6
  328.5 3.7 %slice-start.1 = ((s8[8388608]{0:T(1024)(128)(4,1)}), s8[4194304]{0:T(1024)(128)(4,1)S(1)}, s32[]{:S(2)}) async-start(s8[8388608]{0:T(1024)(128)(4,1)} %bitcast.25), calls=%async_computation.5 | async-start | bytes 8388608
  331.6 3.3 copy-start.1
  (2 other events, 3.3 us)
Sparse Core Ops, SparseCore 0:
  13.2 26.9 reduce-scatter.1
  42.8 169.2 all-gather.2
  214.1 103.7 all-gather.4
where the time goes:
time: 342 us; the launch traced here: 341 us
  waiting for transfers between devices  258 us (75%)
  matrix products  25.5 us (7%)
  local copies, waits for them, and re-layouts  19.2 us (6%)
  between operations  13.5 us (4%)
  starting transfers between devices  12.5 us (4%)
  other arithmetic  12.3 us (4%)
    all_gather x1, waiting for transfers between devices, per_device(): lax.all_gather(ref_vals, 'seq', axis=0, tiled=True)  98.7 us
    ppermute x6, waiting for transfers between devices, from_partner(): return lax.ppermute(block, axis, route)  82 us
    all_gather x1, waiting for transfers between devices, per_device(): lax.all_gather(ref_keys, 'seq', axis=0, tiled=True)  50.6 us
    reduce_scatter x1, waiting for transfers between devices, reference_pair(): lax.psum_scatter(stacked.astype(jnp.bfloat16), 'tensor', scatter_dimensio...  27 us
    dot_general x6, matrix products, attend(): jnp.dot(weights.astype(jnp.bfloat16), values[:, col_start:col_stop], pref...  13.6 us
    unnamed x56, local copies, waits for them, and re-layouts  13.5 us
    ppermute x6, starting transfers between devices, from_partner(): return lax.ppermute(block, axis, route)  12.4 us
    dot_general x6, matrix products, attend(): jnp.einsum('qd,kd->qk', queries[:, col_start:col_stop], key_rows[:, col_s...  8.46 us
  transfers between devices with their start and end apart: 9, of which 7 were waited for; matrix products, arithmetic and copies ran while one was open for 8% of the time, Pallas kernels for 0%

commit v1 on v0

--- a/solution.py
+++ b/solution.py
@@ -6,6 +6,11 @@
 HD = 128
 VIEW_LEN = 4096
 EPSILON = 1e-06
+
+
+def swapped_in(value, name, d):
+    sent = jnp.stack([value] * lax.axis_size(name))
+    return jnp.concatenate(lax.all_to_all(sent, name, 0, 0), axis=d)
 
 
 def from_partner(block, axis, apart):
@@ -97,7 +102,7 @@
     carried = attend(
         carried,
         q_tok,
-        lax.all_gather(ref_keys, "seq", axis=0, tiled=True),
+        swapped_in(ref_keys, "seq", 0),
         lax.all_gather(ref_vals, "seq", axis=0, tiled=True),
     )
     running_max, running_sum, weighted = carried

time: 342 us -> 247 us (0.72)
  waiting for transfers between devices: 258 us -> 151 us
  local copies, waits for them, and re-layouts: 19.2 us -> 24.5 us
  other arithmetic: 12.3 us -> 16.9 us
  starting transfers between devices: 12.5 us -> 16.4 us
    all_gather x1 -> x0, waiting for transfers between devices: 50.6 us -> none  [per_device(): lax.all_gather(ref_keys, 'seq', axis=0, tiled=True)]
    all_gather x1, waiting for transfers between devices: 98.7 us -> 69.5 us  [per_device(): lax.all_gather(ref_vals, 'seq', axis=0, tiled=True)]
    reduce_scatter x1, waiting for transfers between devices: 27 us -> 0.01 us  [reference_pair(): lax.psum_scatter(stacked.astype(jnp.bfloat16), 'tensor', scatter_dimensio...]
    all_to_all x0 -> x1, starting transfers between devices: none -> 9.06 us  [swapped_in(): return jnp.concatenate(lax.all_to_all(sent, name, 0, 0), axis=d)]
    ppermute x6, starting transfers between devices: 12.4 us -> 7.3 us  [from_partner(): return lax.ppermute(block, axis, route)]
    unnamed x56 -> x48, local copies, waits for them, and re-layouts: 13.5 us -> 13.5 us
  transfers between devices with their start and end apart: 9 -> 9, of which waited for: 7 -> 6; matrix products, arithmetic and copies ran while one was open for 8% -> 18% of each run, Pallas kernels for 0% -> 0%
where the time goes in v1:
time: 247 us; the launch traced here: 246 us
  waiting for transfers between devices  151 us (61%)
  local copies, waits for them, and re-layouts  24.5 us (10%)
  matrix products  23.6 us (10%)
  other arithmetic  16.9 us (7%)
  starting transfers between devices  16.4 us (7%)
  between operations  13.7 us (6%)
    ppermute x6, waiting for transfers between devices, from_partner(): return lax.ppermute(block, axis, route)  81.1 us
    all_gather x1, waiting for transfers between devices, per_device(): lax.all_gather(ref_vals, 'seq', axis=0, tiled=True)  69.5 us
    dot_general x6, matrix products, attend(): jnp.dot(weights.astype(jnp.bfloat16), values[:, col_start:col_stop], pref...  13.5 us
    unnamed x48, local copies, waits for them, and re-layouts  13.5 us
    all_to_all x1, starting transfers between devices, swapped_in(): return jnp.concatenate(lax.all_to_all(sent, name, 0, 0), axis=d)  9.06 us
    ppermute x6, starting transfers between devices, from_partner(): return lax.ppermute(block, axis, route)  7.3 us
    reduce_sum x6, other arithmetic, attend(): jnp.sum(weights, axis=1)  6.84 us
    dot_general x6, matrix products, attend(): jnp.einsum('qd,kd->qk', queries[:, col_start:col_stop], key_rows[:, col_s...  5.92 us
  transfers between devices with their start and end apart: 9, of which 6 were waited for; matrix products, arithmetic and copies ran while one was open for 18% of the time, Pallas kernels for 0%

profile of v1, /device:TPU:1, one launch (start us, length us, event | category | flops | bytes accessed | tf_op | source)
XLA Modules:
  0.0 245.8 jit_solution(14278400234809139942)
XLA Ops:
  6.5 3.2 %collective-permute-start = (bf16[512,384]{1,0:T(8,128)(2,1)}, bf16[512,384]{1,0:T(8,128)(2,1)S(1)}, u32[]{:S(2)}, u32[]{:S(2)}) collective-permute-start(bf16[512,384]{1,0:T(8,128)(2,1)} %param.8), channel_id=1, source_target_pairs={{0,4},{4,0},{8,12},{12,8},{16,20},{20,16},{24,28},{28,24},{32,36},... | collective-permute-start | bytes 1179656 | tf_op jit(solution)/shard_map/ppermute | solution.py:23
  9.9 1.5 collective-permute-done
  11.3 2.0 pad_maximum_fusion.2
  13.3 2.0 convolution_convert_fusion.1
  17.4 1.5 collective-permute-start.4
  18.9 2.2 convolution_convert_fusion
  22.5 9.9 %collective-permute-done.1 = bf16[1024,384]{1,0:T(8,128)(2,1)} collective-permute-done((bf16[1024,384]{1,0:T(8,128)(2,1)}, bf16[1024,384]{1,0:T(8,128)(2,1)}, u32[]{:S(2)}, u32[]{:S(2)}) %collective-permute-start.1) | collective-permute-done | bytes 786464 | tf_op jit(solution)/shard_map/ppermute | solution.py:23
  32.4 2.4 pad_maximum_fusion
  34.8 1.2 collective-permute-start.2
  36.0 13.1 %collective-permute-done.4 = bf16[1024,384]{1,0:T(8,128)(2,1)S(1)} collective-permute-done((bf16[1024,384]{1,0:T(8,128)(2,1)S(1)}, bf16[1024,384]{1,0:T(8,128)(2,1)S(1)}, u32[]{:S(2)}, u32[]{:S(2)}) %collective-permute-start.4) | collective-permute-done | bytes 786464 | tf_op jit(solution)/shard_map/ppermute | solution.py:23
  49.1 2.4 pad_maximum_fusion.1
  51.5 1.3 collective-permute-start.5
  54.3 1.3 slice.80
  57.5 1.3 stack.8
  58.8 9.1 %all-to-all-start = ((bf16[64,32,384]{2,1,0:T(8,128)(2,1)}), bf16[64,32,384]{2,1,0:T(8,128)(2,1)S(1)}, u32[]{:S(2)}, u32[]{:S(2)}) async-start(bf16[64,32,384]{2,1,0:T(8,128)(2,1)} %stack.8), calls=%async_computation.1 | async-start | bytes 3145728 | tf_op jit(solution)/shard_map/all_to_all | solution.py:13
  68.7 1.8 constant_dynamic-update-slice_fusion.6
  70.5 2.1 constant_dynamic-update-slice_fusion.1
  73.5 25.7 %collective-permute-done.2 = bf16[2048,384]{1,0:T(8,128)(2,1)} collective-permute-done((bf16[2048,384]{1,0:T(8,128)(2,1)}, bf16[2048,384]{1,0:T(8,128)(2,1)}, u32[]{:S(2)}, u32[]{:S(2)}) %collective-permute-start.2) | collective-permute-done | bytes 1572896 | tf_op jit(solution)/shard_map/ppermute | solution.py:23
  99.2 2.7 %constant_dynamic-update-slice_fusion = bf16[4096,384]{1,0:T(8,128)(2,1)} fusion(bf16[4096,384]{1,0:T(8,128)(2,1)} %constant_dynamic-update-slice_fusion.1, bf16[2048,384]{1,0:T(8,128)(2,1)} %collective-permute-done.2), kind=kLoop, calls=%fused_computation.82 | loop fusion | bytes 3145728 | tf_op jit(solution)/shard_map/concatenate | solution.py:99
  101.9 31.0 %collective-permute-done.5 = bf16[2048,384]{1,0:T(8,128)(2,1)} collective-permute-done((bf16[2048,384]{1,0:T(8,128)(2,1)}, bf16[2048,384]{1,0:T(8,128)(2,1)}, u32[]{:S(2)}, u32[]{:S(2)}) %collective-permute-start.5) | collective-permute-done | bytes 1572896 | tf_op jit(solution)/shard_map/ppermute | solution.py:23
  132.9 2.7 %constant_dynamic-update-slice_fusion.4 = bf16[4096,384]{1,0:T(8,128)(2,1)} fusion(bf16[4096,384]{1,0:T(8,128)(2,1)} %constant_dynamic-update-slice_fusion.5, bf16[2048,384]{1,0:T(8,128)(2,1)} %collective-permute-done.5), kind=kLoop, calls=%fused_computation.86 | loop fusion | bytes 3145728 | tf_op jit(solution)/shard_map/concatenate | solution.py:100
  135.6 1.3 multiply_reduce_fusion
  136.9 1.3 multiply_reduce_fusion.1
  138.2 1.3 multiply_reduce_fusion.2
  140.1 1.5 fusion.4
  142.6 1.5 fusion.2
  145.2 1.4 fusion
  152.6 69.5 %all-gather.2.cloned.1.call-done = bf16[2048,384]{1,0:T(8,128)(2,1)} async-done(((bf16[32,384]{1,0:T(8,128)(2,1)}), bf16[2048,384]{1,0:T(8,128)(2,1)}) %all-gather.2.cloned.1.call-update) | async-done | bytes 1572880 | tf_op jit(solution)/shard_map/all_gather | solution.py:106
  222.0 3.3 %fusion.18 = f32[512,128]{0,1:T(8,128)S(1)} fusion(f32[2048,512]{1,0:T(8,128)} %copy-done.9, f32[512]{0:T(512)S(1)} %get-tuple-element.10, bf16[2048,384]{1,0:T(8,128)(2,1)} %all-gather.2.cloned.1.call-done), kind=kOutput, calls=%fused_computation.29 | convolution fusion | flops 271581184 | bytes 4982784 | tf_op jit(solution)/shard_map/dot_general | solution.py:47
  225.4 5.3 %fusion.54 = f32[512,128]{0,1:T(8,128)S(1)} fusion(f32[512,128]{0,1:T(8,128)S(1)} %fusion.18, f32[4096,512]{1,0:T(8,128)} %copy-done.4, f32[512]{0:T(512)S(1)} %get-tuple-element.14, bf16[4096,384]{1,0:T(8,128)(2,1)} %constant_dynamic-update-slice_fusion.4, f32[512]{0:T(512)S(1)} %get-tuple-element.9, f32[512]{0:T(512)S(1)} %get-tuple-element.13), kind=kOutput, calls=%fused_computation.48 | convolution fusion | flops 543358976 | bytes 9967616 | tf_op jit(solution)/shard_map/dot_general | solution.py:47
  232.6 1.6 fusion.45
  236.3 1.6 fusion.36
  (85 shorter events, 22.3 us)
Async XLA Ops:
  6.5 6.8 %copy-start = (bf16[768,1536]{1,0:T(8,128)(2,1)S(1)}, bf16[768,1536]{1,0:T(8,128)(2,1)}, u32[]{:S(2)}) copy-start(bf16[768,1536]{1,0:T(8,128)(2,1)} %param.11) | copy-start | bytes 7077892
  6.5 9.7 %copy-start.12 = (bf16[512,384]{1,0:T(8,128)(2,1)S(1)}, bf16[512,384]{1,0:T(8,128)(2,1)}, u32[]{:S(2)}) copy-start(bf16[512,384]{1,0:T(8,128)(2,1)} %param.9) | copy-start | bytes 1179652
  6.5 47.8 %reduce-scatter.2.cloned.1.call-start = ((), (), s32[]{:S(2)}) async-start(), calls=%async_computation.2 | async-start | bytes 245760 | tf_op jit(solution)/shard_map/reduce_scatter | solution.py:70
  6.5 4.8 %collective-permute-start = (bf16[512,384]{1,0:T(8,128)(2,1)}, bf16[512,384]{1,0:T(8,128)(2,1)S(1)}, u32[]{:S(2)}, u32[]{:S(2)}) collective-permute-start(bf16[512,384]{1,0:T(8,128)(2,1)} %param.8), channel_id=1, source_target_pairs={{0,4},{4,0},{8,12},{12,8},{16,20},{20,16},{24,28},{28,24},{32,36},... | collective-permute-start | bytes 1179656 | tf_op jit(solution)/shard_map/ppermute | solution.py:23
  9.8 6.5 %collective-permute-start.3 = (bf16[512,384]{1,0:T(8,128)(2,1)}, bf16[512,384]{1,0:T(8,128)(2,1)}, u32[]{:S(2)}, u32[]{:S(2)}) collective-permute-start(bf16[512,384]{1,0:T(8,128)(2,1)} %param.9), channel_id=1, source_target_pairs={{0,4},{4,0},{8,12},{12,8},{16,20},{20,16},{24,28},{28,24},{32,36},... | collective-permute-start | bytes 1179656 | tf_op jit(solution)/shard_map/ppermute | solution.py:23
  13.3 9.2 %copy-start.15 = (f32[128]{0:T(128)S(1)}, f32[128]{0:T(128)}, u32[]{:S(2)}) copy-start(f32[128]{0:T(128)} %param.13) | copy-start | bytes 1540
  13.3 19.1 %copy-start.11 = (bf16[512,384]{1,0:T(8,128)(2,1)S(1)}, bf16[512,384]{1,0:T(8,128)(2,1)}, u32[]{:S(2)}) copy-start(bf16[512,384]{1,0:T(8,128)(2,1)} %param.8) | copy-start | bytes 1179652
  13.3 19.1 %collective-permute-start.1 = (bf16[1024,384]{1,0:T(8,128)(2,1)}, bf16[1024,384]{1,0:T(8,128)(2,1)}, u32[]{:S(2)}, u32[]{:S(2)}) collective-permute-start(bf16[1024,384]{1,0:T(8,128)(2,1)} %pad_maximum_fusion.2), channel_id=1, source_target_pairs={{0,8},{8,0},{4,12},{12,4},{16,24},{24,16},{20,28},{28,20},{32,40},... | collective-permute-start | bytes 2359304 | tf_op jit(solution)/shard_map/ppermute | solution.py:23
  17.4 31.8 %collective-permute-start.4 = (bf16[1024,384]{1,0:T(8,128)(2,1)S(1)}, bf16[1024,384]{1,0:T(8,128)(2,1)S(1)}, u32[]{:S(2)}, u32[]{:S(2)}) collective-permute-start(bf16[1024,384]{1,0:T(8,128)(2,1)S(1)} %pad_maximum_fusion.3), channel_id=1, source_target_pairs={{0,8},{8,0},{4,12},{12,4},{16,24},{24,16},{20,28},{28,20},{32,40},... | collective-permute-start | bytes 2359304 | tf_op jit(solution)/shard_map/ppermute | solution.py:23
  22.4 199.6 %all-gather.2.cloned.1.call-start = ((), (), s32[]{:S(2)}) async-start(), calls=%async_computation.3 | async-start | bytes 1597440 | tf_op jit(solution)/shard_map/all_gather | solution.py:106
  34.8 64.4 %collective-permute-start.2 = (bf16[2048,384]{1,0:T(8,128)(2,1)}, bf16[2048,384]{1,0:T(8,128)(2,1)}, u32[]{:S(2)}, u32[]{:S(2)}) collective-permute-start(bf16[2048,384]{1,0:T(8,128)(2,1)} %pad_maximum_fusion), channel_id=1, source_target_pairs={{0,16},{16,0},{4,20},{20,4},{8,24},{24,8},{12,28},{28,12},{32,48},... | collective-permute-start | bytes 4718600 | tf_op jit(solution)/shard_map/ppermute | solution.py:23
  51.5 81.4 %collective-permute-start.5 = (bf16[2048,384]{1,0:T(8,128)(2,1)}, bf16[2048,384]{1,0:T(8,128)(2,1)}, u32[]{:S(2)}, u32[]{:S(2)}) collective-permute-start(bf16[2048,384]{1,0:T(8,128)(2,1)} %pad_maximum_fusion.1), channel_id=1, source_target_pairs={{0,16},{16,0},{4,20},{20,4},{8,24},{24,8},{12,28},{28,12},{32,48},... | collective-permute-start | bytes 4718600 | tf_op jit(solution)/shard_map/ppermute | solution.py:23
  58.8 87.8 %all-to-all-start = ((bf16[64,32,384]{2,1,0:T(8,128)(2,1)}), bf16[64,32,384]{2,1,0:T(8,128)(2,1)S(1)}, u32[]{:S(2)}, u32[]{:S(2)}) async-start(bf16[64,32,384]{2,1,0:T(8,128)(2,1)} %stack.8), calls=%async_computation.1 | async-start | bytes 3145728 | tf_op jit(solution)/shard_map/all_to_all | solution.py:13
  72.6 63.1 %copy-start.13 = (bf16[512,384]{1,0:T(8,128)(2,1)S(1)}, bf16[512,384]{1,0:T(8,128)(2,1)}, u32[]{:S(2)}) copy-start(bf16[512,384]{1,0:T(8,128)(2,1)} %param.7) | copy-start | bytes 1179652
  101.9 33.7 %copy-start.10 = (bf16[4096,384]{1,0:T(8,128)(2,1)S(1)}, bf16[4096,384]{1,0:T(8,128)(2,1)}, u32[]{:S(2)}) copy-start(bf16[4096,384]{1,0:T(8,128)(2,1)} %constant_dynamic-update-slice_fusion) | copy-start | bytes 9437188
  136.9 3.2 %copy-start.4 = (f32[4096,512]{1,0:T(8,128)}, f32[4096,512]{1,0:T(8,128)S(1)}, u32[]{:S(2)}) copy-start(f32[4096,512]{1,0:T(8,128)S(1)} %get-tuple-element.15) | copy-start | bytes 25165828
  138.2 4.5 %copy-start.3 = (f32[4096,512]{1,0:T(8,128)}, f32[4096,512]{1,0:T(8,128)S(1)}, u32[]{:S(2)}) copy-start(f32[4096,512]{1,0:T(8,128)S(1)} %get-tuple-element.19) | copy-start | bytes 25165828
  139.4 5.7 %copy-start.2 = (f32[4096,512]{1,0:T(8,128)}, f32[4096,512]{1,0:T(8,128)S(1)}, u32[]{:S(2)}) copy-start(f32[4096,512]{1,0:T(8,128)S(1)} %get-tuple-element.23) | copy-start | bytes 25165828
  147.3 2.1 copy-start.9
  148.1 2.5 copy-start.7
  148.8 3.0 %copy-start.5 = (f32[2048,512]{1,0:T(8,128)}, f32[2048,512]{1,0:T(8,128)S(1)}, u32[]{:S(2)}) copy-start(f32[2048,512]{1,0:T(8,128)S(1)} %get-tuple-element.25) | copy-start | bytes 12582916
  222.0 8.7 %copy-start.16 = (bf16[2048,384]{1,0:T(8,128)(2,1)S(1)}, bf16[2048,384]{1,0:T(8,128)(2,1)}, u32[]{:S(2)}) copy-start(bf16[2048,384]{1,0:T(8,128)(2,1)} %all-gather.2.cloned.1.call-done) | copy-start | bytes 4718596
  222.0 9.6 %slice-start.2 = ((s8[8388608]{0:T(1024)(128)(4,1)}), s8[4194304]{0:T(1024)(128)(4,1)S(1)}, s32[]{:S(2)}) async-start(s8[8388608]{0:T(1024)(128)(4,1)} %bitcast.28), calls=%async_computation.6 | async-start | bytes 8388608
  225.4 5.4 %copy-start.8 = (f32[2048,512]{1,0:T(8,128)S(1)}, f32[2048,512]{1,0:T(8,128)}, u32[]{:S(2)}) copy-start(f32[2048,512]{1,0:T(8,128)} %copy-done.7) | copy-start | bytes 12582916
  225.4 6.3 %slice-start.3 = ((s8[8388608]{0:T(1024)(128)(4,1)}), s8[4194304]{0:T(1024)(128)(4,1)S(1)}, s32[]{:S(2)}) async-start(s8[8388608]{0:T(1024)(128)(4,1)} %bitcast.28), calls=%async_computation.7 | async-start | bytes 8388608
  225.4 7.2 %copy-start.14 = (bf16[4096,384]{1,0:T(8,128)(2,1)S(1)}, bf16[4096,384]{1,0:T(8,128)(2,1)}, u32[]{:S(2)}) copy-start(bf16[4096,384]{1,0:T(8,128)(2,1)} %constant_dynamic-update-slice_fusion.4) | copy-start | bytes 9437188
  230.7 4.9 %slice-start = ((s8[8388608]{0:T(1024)(128)(4,1)}), s8[4194304]{0:T(1024)(128)(4,1)S(1)}, s32[]{:S(2)}) async-start(s8[8388608]{0:T(1024)(128)(4,1)} %bitcast.26), calls=%async_computation.4 | async-start | bytes 8388608
  232.6 2.2 copy-start.6
  232.6 3.7 %slice-start.1 = ((s8[8388608]{0:T(1024)(128)(4,1)}), s8[4194304]{0:T(1024)(128)(4,1)S(1)}, s32[]{:S(2)}) async-start(s8[8388608]{0:T(1024)(128)(4,1)} %bitcast.26), calls=%async_computation.5 | async-start | bytes 8388608
  235.7 3.3 %copy-start.1 = (bf16[768,1536]{1,0:T(8,128)(2,1)S(1)}, bf16[768,1536]{1,0:T(8,128)(2,1)}, u32[]{:S(2)}) copy-start(bf16[768,1536]{1,0:T(8,128)(2,1)} %param.11) | copy-start | bytes 7077892
Sparse Core Ops, SparseCore 0:
  22.5 24.6 reduce-scatter.1
  55.8 166.1 all-gather.1
